TPU v7x, 32 devices: a whole 2x2x4 slice. The times are simulated.
32 devices in a mesh: ic: 4 (over z_hi, core), member: 2 (over z_lo), lat: 4 (over y, x).
Axes of the slice: x: 2, y: 2, z: 4 (z_hi: 2, z_lo: 2; z = z_hi * 2 + z_lo), core: 2. Of those that a mesh axis runs over, the one named last changes fastest.
Arguments:
- state: bfloat16 [8, 640, 32, 2560], P(('ic', 'member'), 'lat'), parts along dimension 0, may hold values from -6 to 6
- target: bfloat16 [2560, 32, 2560], P(('ic', 'lat')), parts along dimension 0, may hold values from -6 to 6
- noise: float32 [8, 640, 32, 320], P(('ic', 'member'), 'lat'), parts along dimension 0, may hold values from -4 to 4
- gain: float32 [640, 320], P('lat'), may hold values from 0.2 to 1
- vertical_mix: float32 [32, 32], replicated, may hold values from -1 to 1
Outputs:
- new_state: bfloat16 [8, 640, 32, 2560], P(('ic', 'member'), 'lat'), parts along dimension 0
- crps: float32 [8, 640, 2560], P(('ic', 'member'), 'lat'), parts along dimension 0
There are 4 independent parts, one for each index of `ic`. A program takes and returns all parts, laid end to end along the dimension named above; an argument that names none is the same for every part. Nothing has to cross between parts.
All inputs are finite; a program needn't handle non-finite values.
Results may differ from a plain program's by a relative error of at most 0.0042.
Values may be sent and summed in bfloat16 or wider, within the bound.
A program may use at most 256 MiB of HBM per device.

v0:
```python
import math

import jax
import jax.numpy as jnp
from jax import lax
from jax.sharding import PartitionSpec as P

NLON = 2560
NLAT = 640
MW = 320


def swapped(value, axis, bit):
    mask = 2**bit
    pairs = [(source, source ^ mask) for source in range(lax.axis_size(axis))]
    return lax.ppermute(value, axis, pairs)


def column_info():
    column = jnp.arange(2 * MW, dtype=jnp.int32)
    part = column // MW
    rest = column % MW
    half = MW // 2
    wave = jnp.where(rest < half, 2 * rest + 2 * part, 2 * (rest - half) + 1)
    return (part, wave)


def lon_table():
    part, wave = column_info()
    place = jnp.arange(NLON, dtype=jnp.int32)
    phase = place[:, None] * wave[None, :] % NLON
    angle = phase.astype(jnp.float32) * jnp.float32(2.0 * math.pi / NLON)
    return jnp.where(part[None, :] == 0, jnp.cos(angle), jnp.sin(angle)).astype(jnp.bfloat16)


def lat_basis(is_odd):
    theta = (jnp.arange(NLAT, dtype=jnp.float32) + 0.5) * jnp.float32(math.pi / NLAT)
    modes = jnp.arange(NLAT // 2, dtype=jnp.float32)
    even = jnp.cos(modes[:, None] * theta[None, :])
    odd_basis = jnp.sin((modes[:, None] + 1.0) * theta[None, :])
    return jnp.where(is_odd, odd_basis, even)


def member_score(own, other, truth):
    own = own.astype(jnp.float32)
    other = other.astype(jnp.float32)
    truth = truth.astype(jnp.float32)
    skill = jnp.mean(jnp.abs(own - truth), axis=1)
    spread = jnp.mean(jnp.abs(own - other), axis=1)
    return skill - 0.5 * spread


def body(state, target, noise, gain, vertical_mix):
    field = state[0]
    rows = field.shape[0]
    levels = field.shape[1]
    modes = NLAT // 2
    highest = lax.Precision.HIGHEST
    table = lon_table()
    zonal = jnp.dot(field.reshape(rows * levels, NLON), table, preferred_element_type=jnp.float32)
    zonal = (zonal * jnp.float32(1.0 / math.sqrt(NLON))).reshape(rows, levels, 2 * MW)
    gathered = lax.all_to_all(zonal, "lat", split_axis=2, concat_axis=0, tiled=True)
    width = gathered.shape[2]
    first_col = lax.axis_index("lat") * width
    basis = lat_basis(first_col % MW >= MW // 2)
    spectral = jnp.dot(basis, gathered.reshape(NLAT, levels * width), precision=highest)
    spectral = spectral.reshape(modes, levels, width) * jnp.float32(math.sqrt(2.0 / NLAT))
    forced = gain.T[:, None, :] * spectral + jnp.transpose(noise[0], (2, 1, 0))
    back = jnp.dot(basis.T, forced.reshape(modes, levels * width), precision=highest)
    back = (back.reshape(NLAT, levels, width) * jnp.float32(math.sqrt(2.0 / modes))).astype(
        jnp.bfloat16
    )
    returned = lax.all_to_all(back, "lat", split_axis=0, concat_axis=2, tiled=True)
    tendency = lax.dot_general(
        returned.reshape(rows * levels, 2 * MW),
        table,
        (((1,), (1,)), ((), ())),
        preferred_element_type=jnp.float32,
    )
    tendency = (tendency * jnp.float32(1.0 / math.sqrt(MW))).reshape(rows, levels, NLON)
    mixed = jnp.einsum("ab,jbi->jai", vertical_mix, tendency, precision=highest)
    updated = (field.astype(jnp.float32) + mixed).astype(jnp.bfloat16)
    other = swapped(updated, "member", 0)
    crps = member_score(updated, other, target)[None]
    return (updated[None], crps)


def solution(mesh):
    placed = (
        P(("ic", "member"), "lat", None, None),
        P(("ic", "lat"), None, None),
        P(("ic", "member"), "lat", None, None),
        P("lat", None),
        P(),
    )
    return jax.shard_map(
        body,
        mesh=mesh,
        in_specs=placed,
        out_specs=(P(("ic", "member"), "lat", None, None), P(("ic", "member"), "lat", None)),
        check_vma=False,
    )
```

profile of v0, /device:TPU:0, one launch (start us, length us, event | category | flops | bytes accessed | tf_op | source)
XLA Modules:
  0.0 1314.7 jit_solution(14090977065773513158)
XLA Ops:
  0.6 0.0 copy-start
  0.7 27.1 %select_convert_fusion.8 = bf16[2560,640]{1,0:T(8,128)(2,1)S(1)} fusion(s32[640]{0:T(1024)S(1)} %fusion.34, pred[640]{0:T(1024)(128)(4,1)S(1)} %broadcast_compare_fusion), kind=kLoop, calls=%fused_computation.19.clone.1.clone.1 | loop fusion | flops 18022400 | bytes 3280000 | tf_op jit(solution)/shard_map/dot_general | solution.py:60
  27.8 22.4 %multiply_bitcast_fusion = f32[5120,640]{0,1:T(8,128)} fusion(bf16[5120,2560]{1,0:T(8,128)(2,1)} %bitcast.62, bf16[2560,640]{1,0:T(8,128)(2,1)S(1)} %select_convert_fusion.8), kind=kOutput, calls=%fused_computation.10 | convolution fusion | flops 16780492800 | bytes 42598400 | tf_op jit(solution)/shard_map/dot_general | solution.py:60
  50.2 14.0 %copy.19 = f32[5120,640]{1,0:T(8,128)} copy(f32[5120,640]{0,1:T(8,128)} %multiply_bitcast_fusion) | data formatting | bytes 26214400 | tf_op jit(solution)/shard_map/mul | solution.py:61
  64.2 22.5 %copy.20 = f32[160,32,640]{0,1,2:T(8,128)} copy(f32[160,32,640]{2,1,0:T(8,128)} %bitcast.61) | data formatting | bytes 26214400 | tf_op jit(solution)/shard_map/reshape | solution.py:61
  86.7 0.0 copy-start.1
  86.7 8.3 all-to-all-start
  95.1 0.0 copy-done.1
  95.1 228.7 %all-to-all-done = f32[160,32,640]{0,1,2:T(8,128)} async-done(((f32[160,32,640]{0,1,2:T(8,128)}), f32[160,32,640]{0,1,2:T(8,128)}, u32[]{:S(2)}, u32[]{:S(2)}) %all-to-all-start) | async-done | bytes 13107232 | tf_op jit(solution)/shard_map/all_to_all | solution.py:62
  323.8 25.6 %copy.21 = f32[4,160,32,160]{1,0,3,2:T(4,128)} copy(f32[4,160,32,160]{1,2,3,0:T(8,128)} %bitcast.6) | data formatting | bytes 26214400 | tf_op jit(solution)/shard_map/all_to_all | solution.py:62
  349.3 21.7 %reshape.89 = f32[640,5120]{0,1:T(8,128)} reshape(f32[4,160,32,160]{1,0,3,2:T(4,128)} %copy.21) | data formatting | bytes 26214400 | tf_op jit(solution)/shard_map/reshape | solution.py:66
  371.1 38.3 %fusion.15 = f32[320,32,160]{0,2,1:T(8,128)S(1)} fusion(f32[32,160,640]{2,1,0:T(8,128)} %bitcast.60, f32[640]{0:T(1024)S(1)} %add_multiply_fusion, f32[320]{0:T(512)S(1)} %iota_add_fusion, pred[]{:T(512)S(6)} %ge.3), kind=kOutput, calls=%fused_computation.27 | convolution fusion | flops 12583526400 | bytes 19664640 | tf_op jit(solution)/shard_map/dot_general | solution.py:66
  409.4 56.2 %multiply_convert_fusion = bf16[640,32,160]{0,2,1:T(8,128)(2,1)} fusion(f32[1,160,32,320]{3,2,1,0:T(8,128)} %param.7, f32[320,32,160]{0,2,1:T(8,128)S(1)} %fusion.15, f32[320,160]{0,1:T(8,128)S(1)} %multiply_bitcast_fusion.1, f32[640]{0:T(1024)S(1)} %add_multiply_fusion, f32[320]{0:T(512)S(1)} %iota_add_fusion, pred[]{:T(512)S(6)} %ge.3), kind=kOutput, calls=%fused_computation.9 | convolution fusion | flops 12593356800 | bytes 19869440 | tf_op jit(solution)/shard_map/dot_general | solution.py:69
  465.5 15.9 %copy.23 = bf16[640,32,160]{2,1,0:T(8,128)(2,1)} copy(bf16[640,32,160]{0,2,1:T(8,128)(2,1)} %multiply_convert_fusion) | data formatting | bytes 13107200 | tf_op jit(solution)/shard_map/convert_element_type | solution.py:70
  481.5 6.0 all-to-all-start.1
  487.5 28.3 %select_convert_fusion.7 = bf16[2560,640]{1,0:T(8,128)(2,1)} fusion(s32[640]{0:T(1024)S(1)} %fusion.34, pred[640]{0:T(1024)(128)(4,1)S(1)} %broadcast_compare_fusion), kind=kLoop, calls=%fused_computation.19.clone.clone.1 | loop fusion | flops 18022400 | bytes 3280000 | tf_op jit(solution)/shard_map/dot_general | solution.py:74
  515.8 86.2 %all-to-all-done.1 = bf16[640,32,160]{2,1,0:T(8,128)(2,1)} async-done(((bf16[640,32,160]{2,1,0:T(8,128)(2,1)}), bf16[640,32,160]{2,1,0:T(8,128)(2,1)}, u32[]{:S(2)}, u32[]{:S(2)}) %all-to-all-start.1) | async-done | bytes 6553632 | tf_op jit(solution)/shard_map/all_to_all | solution.py:73
  602.0 13.3 %copy.30 = bf16[4,160,32,160]{3,0,2,1:T(4,128)(2,1)} copy(bf16[4,160,32,160]{3,2,1,0:T(8,128)(2,1)} %bitcast.15) | data formatting | bytes 13107200 | tf_op jit(solution)/shard_map/all_to_all | solution.py:73
  615.3 0.0 copy-start.2
  615.3 15.4 %reshape.91 = bf16[5120,640]{1,0:T(8,128)(2,1)} reshape(bf16[160,32,4,160]{3,2,1,0:T(4,128)(2,1)} %bitcast.63) | data formatting | bytes 13107200 | tf_op jit(solution)/shard_map/reshape | solution.py:75
  630.7 0.0 copy-done.2
  630.7 28.4 %convolution_multiply_fusion = f32[5120,2560]{1,0:T(8,128)} fusion(bf16[5120,640]{1,0:T(8,128)(2,1)} %reshape.91, bf16[2560,640]{1,0:T(8,128)(2,1)S(1)} %copy-done.2), kind=kOutput, calls=%fused_computation.8 | convolution fusion | flops 16790323200 | bytes 62259200 | tf_op jit(solution)/shard_map/dot_general | solution.py:74
  659.1 0.0 copy-done
  659.1 58.3 %fusion.4 = bf16[160,32,2560]{2,1,0:T(8,128)(2,1)} fusion(bf16[1,160,32,2560]{3,2,1,0:T(8,128)(2,1)} %param.5, f32[160,32,2560]{2,1,0:T(8,128)} %bitcast.59, f32[32,32]{1,0:T(8,128)S(1)} %copy-done), kind=kOutput, calls=%fused_computation.7 | convolution fusion | flops 5072486400 | bytes 104861696 | tf_op jit(solution)/shard_map/ab,jbi->jai/dot_general | solution.py:81
  717.4 1.6 collective-permute-start
  718.9 562.2 %collective-permute-done = bf16[160,32,2560]{2,1,0:T(8,128)(2,1)} collective-permute-done((bf16[160,32,2560]{2,1,0:T(8,128)(2,1)}, bf16[160,32,2560]{2,1,0:T(8,128)(2,1)}, u32[]{:S(2)}, u32[]{:S(2)}) %collective-permute-start) | collective-permute-done | bytes 26214432 | tf_op jit(solution)/shard_map/ppermute | solution.py:16
  1281.1 32.0 %fusion.1 = (f32[160,2560]{1,0:T(8,128)S(1)}, f32[160,2560]{1,0:T(8,128)S(1)}) fusion(bf16[160,32,2560]{2,1,0:T(8,128)(2,1)} %fusion.4, bf16[160,32,2560]{2,1,0:T(8,128)(2,1)} %param.6, bf16[160,32,2560]{2,1,0:T(8,128)(2,1)} %collective-permute-done), kind=kLoop, calls=%fused_computation.3 | loop fusion | flops 117145600 | bytes 81920000 | tf_op jit(solution)/shard_map/reduce_sum | solution.py:48
  1313.1 1.4 subtract_bitcast_fusion
  (5 shorter events, 0.1 us)
Async XLA Ops:
  0.6 658.5 %copy-start = (f32[32,32]{1,0:T(8,128)S(1)}, f32[32,32]{1,0:T(8,128)}, u32[]{:S(2)}) copy-start(f32[32,32]{1,0:T(8,128)} %param.9) | copy-start | bytes 12292
  86.7 8.3 copy-start.1
  86.7 237.1 %all-to-all-start = ((f32[160,32,640]{0,1,2:T(8,128)}), f32[160,32,640]{0,1,2:T(8,128)}, u32[]{:S(2)}, u32[]{:S(2)}) async-start(f32[160,32,640]{0,1,2:T(8,128)} %copy.20), calls=%async_computation | async-start | bytes 41943040 | tf_op jit(solution)/shard_map/all_to_all | solution.py:62
  481.5 120.5 %all-to-all-start.1 = ((bf16[640,32,160]{2,1,0:T(8,128)(2,1)}), bf16[640,32,160]{2,1,0:T(8,128)(2,1)}, u32[]{:S(2)}, u32[]{:S(2)}) async-start(bf16[640,32,160]{2,1,0:T(8,128)(2,1)} %copy.23), calls=%async_computation.1 | async-start | bytes 20971520 | tf_op jit(solution)/shard_map/all_to_all | solution.py:73
  615.3 15.5 %copy-start.2 = (bf16[2560,640]{1,0:T(8,128)(2,1)S(1)}, bf16[2560,640]{1,0:T(8,128)(2,1)}, u32[]{:S(2)}) copy-start(bf16[2560,640]{1,0:T(8,128)(2,1)} %select_convert_fusion.7) | copy-start | bytes 9830404
  717.4 563.7 %collective-permute-start = (bf16[160,32,2560]{2,1,0:T(8,128)(2,1)}, bf16[160,32,2560]{2,1,0:T(8,128)(2,1)}, u32[]{:S(2)}, u32[]{:S(2)}) collective-permute-start(bf16[160,32,2560]{2,1,0:T(8,128)(2,1)} %fusion.4), channel_id=1, source_target_pairs={{0,4},{4,0},{1,5},{5,1},{2,6},{6,2},{3,7},{7,3},{8,12},{12,8},{9,1... | collective-permute-start | bytes 78643208 | tf_op jit(solution)/shard_map/ppermute | solution.py:16
where the time goes:
time: 1320 us; the launch traced here: 1310 us
  waiting for transfers between devices  877 us (66%)
  matrix products  204 us (15%)
  local copies, waits for them, and re-layouts  128 us (10%)
  other arithmetic  88.9 us (7%)
  starting transfers between devices  15.8 us (1%)
    ppermute x1, waiting for transfers between devices, swapped(): return lax.ppermute(value, axis, pairs)  562 us
    all_to_all x1, waiting for transfers between devices, body(): lax.all_to_all(zonal, 'lat', split_axis=2, concat_axis=0, tiled=True)  229 us
    all_to_all x1, waiting for transfers between devices, body(): lax.all_to_all(back, 'lat', split_axis=0, concat_axis=2, tiled=True)  86.2 us
    dot_general x1, matrix products, body(): mixed = jnp.einsum('ab,jbi->jai', vertical_mix, tendency, precision=highest)  58.3 us
    dot_general x1, matrix products, body(): jnp.dot(basis.T, forced.reshape(modes, levels * width), precision=highest)  56.2 us
    dot_general x1, matrix products, body(): jnp.dot(basis, gathered.reshape(NLAT, levels * width), precision=highest)  38.3 us
    reduce_sum x1, other arithmetic, member_score(): skill = jnp.mean(jnp.abs(own - truth), axis=1)  32 us
    dot_general x1, matrix products, body(): lax.dot_general(returned.reshape(rows * levels, 2 * MW), table, (((1,), (...  28.4 us
  transfers between devices with their start and end apart: 3, of which 3 were waited for; matrix products, arithmetic and copies ran while one was open for 2% of the time, Pallas kernels for 0%

commit v1 on v0

v1 whole, which is shorter than its diff:
```python
import math

import jax
import jax.numpy as jnp
from jax import lax
from jax.sharding import PartitionSpec as P


def swapped(value):
    return lax.ppermute(value, "member", [(0, 1), (1, 0)])


def column_info(mw):
    column = jnp.arange(2 * mw, dtype=jnp.int32)
    part = column // mw
    rest = column % mw
    half = mw // 2
    return part, jnp.where(rest < half, 2 * rest + 2 * part, 2 * (rest - half) + 1)


def lon_table(nlon, mw):
    part, wave = column_info(mw)
    inner = math.gcd(nlon, 64)
    outer = nlon // inner

    def angles(step, count):
        phase = (step * jnp.arange(count, dtype=jnp.int32))[:, None] * wave[None, :] % nlon
        angle = phase.astype(jnp.float32) * jnp.float32(2.0 * math.pi / nlon)
        return jnp.cos(angle), jnp.sin(angle)

    ca, sa = angles(inner, outer)
    cb, sb = angles(1, inner)
    sine = part[None, :] != 0
    first = jnp.where(sine, sa, ca)
    second = jnp.where(sine, ca, -sa)
    first, second, cb, sb = lax.optimization_barrier((first, second, cb, sb))
    table = first[:, None, :] * cb[None] + second[:, None, :] * sb[None]
    return lax.optimization_barrier(table.reshape(nlon, 2 * mw).astype(jnp.bfloat16))


def lat_basis(nlat, modes, is_odd):
    theta = (jnp.arange(nlat, dtype=jnp.float32) + 0.5) * jnp.float32(math.pi / nlat)
    k = jnp.arange(modes, dtype=jnp.float32)
    shift = jnp.where(is_odd, jnp.float32(1.0), jnp.float32(0.0))
    angle = (k[:, None] + shift) * theta[None, :]
    basis = jnp.where(is_odd, jnp.sin(angle), jnp.cos(angle))
    return lax.optimization_barrier(basis)


def body(state, target, noise, gain, vertical_mix):
    field = state[0]
    rows, levels, nlon = field.shape
    width, modes = gain.shape
    n = lax.axis_size("lat")
    nlat = rows * n
    mw = width * n // 2
    half = rows // 2
    f32, bf16 = jnp.float32, jnp.bfloat16
    high = lax.Precision.HIGH
    me = lax.axis_index("member")
    mine, theirs = me * half, (1 - me) * half

    other_state = swapped(lax.dynamic_slice_in_dim(field, theirs, half, 0))

    table = lon_table(nlon, mw)
    zonal = jnp.dot(field.reshape(rows * levels, nlon), table, preferred_element_type=f32)
    zonal = (zonal * f32(1.0 / math.sqrt(nlon))).astype(bf16)
    zonal = zonal.reshape(rows, levels, n, width).transpose(2, 0, 3, 1)
    zonal = zonal.reshape(n, rows, width * levels)
    gathered = lax.all_to_all(zonal, "lat", 0, 0, tiled=True).reshape(nlat, width * levels)

    odd = (lax.axis_index("lat") * width) % mw >= mw // 2
    basis = lat_basis(nlat, modes, odd)
    basis_hi = basis.astype(bf16)
    basis_lo = (basis - basis_hi.astype(f32)).astype(bf16)
    spectral = jnp.dot(basis_hi, gathered, preferred_element_type=f32) + jnp.dot(
        basis_lo, gathered, preferred_element_type=f32
    )
    gains = jnp.repeat(gain.T * f32(math.sqrt(2.0 / nlat)), levels, axis=1)
    forcing = noise[0].reshape(width * levels, modes).T
    gains, forcing = lax.optimization_barrier((gains, forcing))
    forced = gains * spectral + forcing
    back = jnp.dot(basis.T, forced, precision=high) * f32(math.sqrt(2.0 / modes))
    back = back.astype(bf16).reshape(n, rows, width * levels)
    returned = lax.all_to_all(back, "lat", 0, 0, tiled=True)
    returned = returned.reshape(n, rows, width, levels).transpose(1, 3, 0, 2)
    returned = returned.reshape(rows, levels, n * width)
    mixed = jnp.einsum("ab,jbc->jac", vertical_mix * f32(1.0 / math.sqrt(mw)), returned.astype(f32), precision=high)
    mixed = lax.optimization_barrier(mixed.astype(bf16))
    other_mixed = swapped(lax.dynamic_slice_in_dim(mixed, theirs, half, 0))

    def advance(start, coefficients):
        count = start.shape[0]
        move = lax.dot_general(
            coefficients.reshape(count * levels, n * width),
            table,
            (((1,), (1,)), ((), ())),
            preferred_element_type=f32,
        )
        flat = start.reshape(count * levels, nlon).astype(f32)
        return (flat + move).astype(bf16).reshape(count, levels, nlon)

    updated = advance(field, mixed)
    skill = jnp.mean(jnp.abs(updated.astype(f32) - target.astype(f32)), axis=1)
    other = advance(other_state, other_mixed)
    own = lax.dynamic_slice_in_dim(updated, mine, half, 0)
    spread = 0.5 * jnp.mean(jnp.abs(own.astype(f32) - other.astype(f32)), axis=1)
    far = swapped(spread)
    first = jnp.where(me == 0, spread, far)
    second = jnp.where(me == 0, far, spread)
    crps = skill - jnp.concatenate([first, second], axis=0)
    return (updated[None], crps[None])


def solution(mesh):
    placed = (
        P(("ic", "member"), "lat", None, None),
        P(("ic", "lat"), None, None),
        P(("ic", "member"), "lat", None, None),
        P("lat", None),
        P(),
    )
    return jax.shard_map(
        body,
        mesh=mesh,
        in_specs=placed,
        out_specs=(P(("ic", "member"), "lat", None, None), P(("ic", "member"), "lat", None)),
        check_vma=False,
    )
```

time: 1320 us -> 527 us (0.40)
  waiting for transfers between devices: 877 us -> 225 us
  matrix products: 204 us -> 104 us
  other arithmetic: 88.9 us -> 39.3 us
    ppermute x1 -> x3, waiting for transfers between devices: 562 us -> 116 us  [swapped(): return lax.ppermute(value, 'member', [(0, 1), (1, 0)])]
    all_to_all x2, waiting for transfers between devices: 315 us -> 109 us  [the longest x1 72.4 us: body(): returned = lax.all_to_all(back, 'lat', 0, 0, tiled=True)]
    dot_general x5 -> x7, matrix products: 204 us -> 104 us  [the longest x2 46 us: advance(): lax.dot_general(coefficients.reshape(count * levels, n * width), table, (...]
    dot_general x2 -> x0, other arithmetic: 55.5 us -> none  [the longest x1 28.3 us: body(): lax.dot_general(returned.reshape(rows * levels, 2 * MW), table, (((1,), (...]
    all_to_all x2 -> x1, local copies, waits for them, and re-layouts: 38.8 us -> 11.4 us  [body(): returned = lax.all_to_all(back, 'lat', 0, 0, tiled=True)]
    transpose x0 -> x1, local copies, waits for them, and re-layouts: none -> 27.1 us  [body(): zonal = zonal.reshape(rows, levels, n, width).transpose(2, 0, 3, 1)]
    reshape x3, local copies, waits for them, and re-layouts: 59.7 us -> 43.9 us  [the longest x1 17 us: body(): returned = returned.reshape(rows, levels, n * width)]
    mul x1 -> x0, local copies, waits for them, and re-layouts: 14 us -> none  [body(): zonal * jnp.float32(1.0 / math.sqrt(NLON))]
  transfers between devices with their start and end apart: 3 -> 5, of which waited for: 3 -> 3; matrix products, arithmetic and copies ran while one was open for 2% -> 29% of each run, Pallas kernels for 0% -> 0%
where the time goes in v1:
time: 527 us; the launch traced here: 517 us
  waiting for transfers between devices  225 us (43%)
  local copies, waits for them, and re-layouts  130 us (25%)
  matrix products  104 us (20%)
  other arithmetic  39.3 us (7%)
  starting transfers between devices  17.6 us (3%)
    ppermute x3, waiting for transfers between devices, swapped(): return lax.ppermute(value, 'member', [(0, 1), (1, 0)])  116 us
    all_to_all x1, waiting for transfers between devices, body(): returned = lax.all_to_all(back, 'lat', 0, 0, tiled=True)  72.4 us
    dot_general x2, matrix products, advance(): lax.dot_general(coefficients.reshape(count * levels, n * width), table, (...  46 us
    all_to_all x1, waiting for transfers between devices, body(): lax.all_to_all(zonal, 'lat', 0, 0, tiled=True).reshape(nlat, width * levels)  36.2 us
    transpose x1, local copies, waits for them, and re-layouts, body(): zonal = zonal.reshape(rows, levels, n, width).transpose(2, 0, 3, 1)  27.1 us
    dot_general x1, matrix products, body(): jnp.dot(field.reshape(rows * levels, nlon), table, preferred_element_type...  23.3 us
    reduce_sum x1, other arithmetic, body(): skill = jnp.mean(jnp.abs(updated.astype(f32) - target.astype(f32)), axis=1)  19.5 us
    reshape x1, local copies, waits for them, and re-layouts, body(): returned = returned.reshape(rows, levels, n * width)  17 us
  transfers between devices with their start and end apart: 5, of which 3 were waited for; matrix products, arithmetic and copies ran while one was open for 29% of the time, Pallas kernels for 0%

profile of v1, /device:TPU:0, one launch (start us, length us, event | category | flops | bytes accessed | tf_op | source)
XLA Modules:
  0.0 516.8 jit_solution(6572821640035002389)
XLA Ops:
  0.7 0.7 fusion.15
  1.4 0.5 negate_select_fusion
  1.9 1.1 add_convert_fusion.1
  2.9 0.0 copy-start.2
  2.9 1.7 copy-done.2
  4.7 23.3 %fusion.3 = bf16[5120,640]{0,1:T(8,128)(2,1)} fusion(bf16[2560,640]{1,0:T(8,128)(2,1)S(1)} %bitcast.67, bf16[5120,2560]{1,0:T(8,128)(2,1)} %bitcast.65), kind=kOutput, calls=%fused_computation.10 | convolution fusion | flops 16783769600 | bytes 36044800 | tf_op jit(solution)/shard_map/dot_general | solution.py:66
  28.0 9.5 %copy.27 = bf16[5120,640]{1,0:T(8,128)(2,1)} copy(bf16[5120,640]{0,1:T(8,128)(2,1)} %fusion.3) | data formatting | bytes 13107200 | tf_op jit(solution)/shard_map/convert_element_type | solution.py:67
  37.5 15.2 %reshape.135 = bf16[160,32,4,160]{3,2,1,0:T(4,128)(2,1)} reshape(bf16[5120,640]{1,0:T(8,128)(2,1)} %copy.27) | data formatting | bytes 13107200 | tf_op jit(solution)/shard_map/reshape | solution.py:68
  52.7 27.1 %copy.28 = bf16[4,160,160,32]{1,3,2,0:T(8,128)(2,1)} copy(bf16[4,160,160,32]{2,0,3,1:T(4,128)(2,1)} %bitcast.54) | data formatting | bytes 13107200 | tf_op jit(solution)/shard_map/transpose | solution.py:68
  79.8 11.6 %copy.29 = bf16[4,160,5120]{2,1,0:T(8,128)(2,1)} copy(bf16[4,160,5120]{1,2,0:T(8,128)(2,1)} %bitcast.55) | data formatting | bytes 13107200 | tf_op jit(solution)/shard_map/reshape | solution.py:69
  91.4 5.7 %all-to-all-start = ((bf16[4,160,5120]{2,1,0:T(8,128)(2,1)}), bf16[4,160,5120]{2,1,0:T(8,128)(2,1)}, u32[]{:S(2)}, u32[]{:S(2)}) async-start(bf16[4,160,5120]{2,1,0:T(8,128)(2,1)} %copy.29), calls=%async_computation | async-start | bytes 13107200 | tf_op jit(solution)/shard_map/all_to_all | solution.py:70
  97.2 10.8 %dynamic-slice_bitcast_fusion = bf16[80,32,2560]{2,1,0:T(8,128)(2,1)} fusion(bf16[1,160,32,2560]{3,2,1,0:T(8,128)(2,1)} %param.5, s32[]{:T(128)S(6)} %select_n.121), kind=kLoop, calls=%fused_computation.7 | loop fusion | bytes 26214404 | tf_op jit(solution)/shard_map/dynamic_slice | solution.py:63
  108.0 3.1 collective-permute-start
  111.1 2.9 fusion.7
  114.0 0.0 copy-start.4
  114.0 8.7 %copy.26 = f32[5120,320]{0,1:T(8,128)} copy(f32[5120,320]{1,0:T(8,128)} %bitcast.64) | data formatting | bytes 13107200 | tf_op jit(solution)/shard_map/reshape;squeeze | solution.py:80
  122.7 0.0 copy-done.4
  122.7 3.7 broadcast_in_dim.15
  126.4 8.7 %copy.30 = f32[320,5120]{1,0:T(8,128)} copy(f32[320,5120]{0,1:T(8,128)} %bitcast.61) | data formatting | bytes 13107200 | tf_op jit(solution)/shard_map/optimization_barrier | solution.py:81
  135.2 36.2 %all-to-all-done = bf16[4,160,5120]{2,1,0:T(8,128)(2,1)} async-done(((bf16[4,160,5120]{2,1,0:T(8,128)(2,1)}), bf16[4,160,5120]{2,1,0:T(8,128)(2,1)}, u32[]{:S(2)}, u32[]{:S(2)}) %all-to-all-start) | async-done | bytes 6553632 | tf_op jit(solution)/shard_map/all_to_all | solution.py:70
  171.4 7.6 %fusion.9 = f32[320,5120]{1,0:T(8,128)} fusion(bf16[640,5120]{1,0:T(8,128)(2,1)} %bitcast.9, f32[320,640]{1,0:T(8,128)S(1)} %fusion.7), kind=kOutput, calls=%fused_computation.28 | convolution fusion | flops 2097356800 | bytes 13926400 | tf_op jit(solution)/shard_map/dot_general | solution.py:76
  179.1 0.0 slice-done
  179.1 0.0 slice-done.1
  179.1 0.0 copy-done
  179.1 7.7 %fusion.5 = f32[320,5120]{1,0:T(8,128)S(1)} fusion(f32[320,5120]{1,0:T(8,128)S(1)} %bitcast.59, f32[320,5120]{1,0:T(8,128)S(1)} %copy-done, f32[320,5120]{1,0:T(8,128)} %fusion.9, bf16[640,5120]{1,0:T(8,128)(2,1)} %bitcast.9, f32[320,640]{1,0:T(8,128)S(1)} %fusion.7), kind=kOutput, calls=%fused_computation.14 | convolution fusion | flops 2102886400 | bytes 33587200 | tf_op jit(solution)/shard_map/dot_general | solution.py:76
  186.8 12.5 %multiply_convert_fusion = bf16[640,5120]{1,0:T(8,128)(2,1)} fusion(f32[320,640]{1,0:T(8,128)S(1)} %fusion.7, f32[320,5120]{1,0:T(8,128)S(1)} %fusion.5), kind=kOutput, calls=%fused_computation.8 | convolution fusion | flops 6298009600 | bytes 13926400 | tf_op jit(solution)/shard_map/dot_general | solution.py:83
  199.3 5.4 %all-to-all-start.1 = ((bf16[4,160,5120]{2,1,0:T(8,128)(2,1)}), bf16[4,160,5120]{2,1,0:T(8,128)(2,1)}, u32[]{:S(2)}, u32[]{:S(2)}) async-start(bf16[4,160,5120]{2,1,0:T(8,128)(2,1)} %bitcast.60), calls=%async_computation.1 | async-start | bytes 13107200 | tf_op jit(solution)/shard_map/all_to_all | solution.py:85
  204.8 72.4 %all-to-all-done.1 = bf16[4,160,5120]{2,1,0:T(8,128)(2,1)} async-done(((bf16[4,160,5120]{2,1,0:T(8,128)(2,1)}), bf16[4,160,5120]{2,1,0:T(8,128)(2,1)}, u32[]{:S(2)}, u32[]{:S(2)}) %all-to-all-start.1) | async-done | bytes 6553632 | tf_op jit(solution)/shard_map/all_to_all | solution.py:85
  277.1 11.4 %copy.31 = bf16[4,160,5120]{1,2,0:T(8,128)(2,1)} copy(bf16[4,160,5120]{2,1,0:T(8,128)(2,1)} %all-to-all-done.1) | data formatting | bytes 13107200 | tf_op jit(solution)/shard_map/all_to_all | solution.py:85
  288.6 17.0 %copy.33 = bf16[160,32,640]{2,1,0:T(8,128)(2,1)} copy(bf16[160,32,640]{0,1,2:T(8,128)(2,1)} %bitcast.56) | data formatting | bytes 13107200 | tf_op jit(solution)/shard_map/reshape | solution.py:87
  305.6 0.0 copy-done.5
  305.6 6.4 %fusion.6 = bf16[160,32,640]{2,1,0:T(8,128)(2,1)S(1)} fusion(bf16[160,32,640]{2,1,0:T(8,128)(2,1)} %copy.33, f32[32,32]{1,0:T(8,128)S(1)} %copy-done.5), kind=kOutput, calls=%fused_computation.16 | convolution fusion | flops 632423424 | bytes 13111296 | tf_op jit(solution)/shard_map/ab,jbc->jac/dot_general | solution.py:88
  312.0 0.0 copy-start.1
  312.1 2.7 copy-done.1
  314.8 2.0 constant_dynamic-slice_fusion
  316.7 1.6 collective-permute-start.1
  318.3 0.0 copy-done.3
  318.3 28.5 %add_convert_fusion = bf16[5120,2560]{1,0:T(8,128)(2,1)} fusion(bf16[5120,2560]{1,0:T(8,128)(2,1)} %bitcast.66, bf16[5120,640]{1,0:T(8,128)(2,1)} %bitcast.62, bf16[2560,640]{1,0:T(8,128)(2,1)S(1)} %bitcast.68), kind=kOutput, calls=%fused_computation.1 | convolution fusion | flops 16816537600 | bytes 62259200 | tf_op jit(solution)/shard_map/dot_general | solution.py:94
  346.8 116.3 %collective-permute-done.1 = bf16[80,32,640]{2,1,0:T(8,128)(2,1)} collective-permute-done((bf16[80,32,640]{2,1,0:T(8,128)(2,1)}, bf16[80,32,640]{2,1,0:T(8,128)(2,1)}, u32[]{:S(2)}, u32[]{:S(2)}) %collective-permute-start.1) | collective-permute-done | bytes 3276832 | tf_op jit(solution)/shard_map/ppermute | solution.py:10
  463.2 0.0 collective-permute-done
  463.2 17.5 %fusion.2 = bf16[2560,2560]{1,0:T(8,128)(2,1)} fusion(bf16[80,32,2560]{2,1,0:T(8,128)(2,1)} %collective-permute-done, bf16[2560,640]{1,0:T(8,128)(2,1)} %bitcast.22, bf16[2560,640]{1,0:T(8,128)(2,1)S(1)} %bitcast.69), kind=kOutput, calls=%fused_computation.6 | convolution fusion | flops 8408268800 | bytes 32768000 | tf_op jit(solution)/shard_map/dot_general | solution.py:94
  480.7 12.9 %fusion.1 = f32[80,2560]{1,0:T(8,128)S(1)} fusion(bf16[80,32,2560]{2,1,0:T(8,128)(2,1)} %bitcast.63, bf16[160,32,2560]{2,1,0:T(8,128)(2,1)} %bitcast.51, s32[]{:T(128)S(6)} %select_n.120), kind=kLoop, calls=%fused_computation.4 | loop fusion | flops 32563200 | bytes 27033604 | tf_op jit(solution)/shard_map/reduce_sum | solution.py:107
  493.6 0.1 broadcast_multiply_fusion
  493.7 1.8 collective-permute-start.2
  495.5 19.5 %abs_reduce_fusion = f32[160,2560]{1,0:T(8,128)S(1)} fusion(bf16[160,32,2560]{2,1,0:T(8,128)(2,1)} %param.6, bf16[160,32,2560]{2,1,0:T(8,128)(2,1)} %bitcast.52), kind=kLoop, calls=%fused_computation | loop fusion | flops 65126400 | bytes 54067200 | tf_op jit(solution)/shard_map/reduce_sum | solution.py:104
  515.0 0.0 collective-permute-done.2
  515.0 0.2 select_bitcast_fusion.1
  515.2 1.4 maximum_subtract_fusion
  (12 shorter events, 0.1 us)
Async XLA Ops:
  2.9 1.7 copy-start.2
  91.4 80.0 %all-to-all-start = ((bf16[4,160,5120]{2,1,0:T(8,128)(2,1)}), bf16[4,160,5120]{2,1,0:T(8,128)(2,1)}, u32[]{:S(2)}, u32[]{:S(2)}) async-start(bf16[4,160,5120]{2,1,0:T(8,128)(2,1)} %copy.29), calls=%async_computation | async-start | bytes 13107200 | tf_op jit(solution)/shard_map/all_to_all | solution.py:70
  108.0 355.2 %collective-permute-start = (bf16[80,32,2560]{2,1,0:T(8,128)(2,1)}, bf16[80,32,2560]{2,1,0:T(8,128)(2,1)}, u32[]{:S(2)}, u32[]{:S(2)}) collective-permute-start(bf16[80,32,2560]{2,1,0:T(8,128)(2,1)} %dynamic-slice_bitcast_fusion), channel_id=1, source_target_pairs={{0,4},{4,0},{1,5},{5,1},{2,6},{6,2},{3,7},{7,3},{8,12},{12,8},{9,1... | collective-permute-start | bytes 39321608 | tf_op jit(solution)/shard_map/ppermute | solution.py:10
  114.0 8.7 %copy-start.4 = (f32[160,320]{1,0:T(8,128)S(1)}, f32[160,320]{1,0:T(8,128)}, u32[]{:S(2)}) copy-start(f32[160,320]{1,0:T(8,128)} %param.8) | copy-start | bytes 614404
  126.4 52.6 %slice-start = ((s8[6553600]{0:T(1024)(128)(4,1)}), s8[2359296]{0:T(1024)(128)(4,1)S(1)}, s32[]{:S(2)}) async-start(s8[6553600]{0:T(1024)(128)(4,1)} %bitcast.57), calls=%async_computation.2 | async-start | bytes 4718592
  171.4 7.6 %slice-start.1 = ((s8[6553600]{0:T(1024)(128)(4,1)}), s8[4194304]{0:T(1024)(128)(4,1)S(1)}, s32[]{:S(2)}) async-start(s8[6553600]{0:T(1024)(128)(4,1)} %bitcast.57), calls=%async_computation.3 | async-start | bytes 8388608
  171.4 7.6 %copy-start = (f32[320,5120]{1,0:T(8,128)S(1)}, f32[320,5120]{1,0:T(8,128)}, u32[]{:S(2)}) copy-start(f32[320,5120]{1,0:T(8,128)} %copy.30) | copy-start | bytes 19660804
  199.3 77.8 %all-to-all-start.1 = ((bf16[4,160,5120]{2,1,0:T(8,128)(2,1)}), bf16[4,160,5120]{2,1,0:T(8,128)(2,1)}, u32[]{:S(2)}, u32[]{:S(2)}) async-start(bf16[4,160,5120]{2,1,0:T(8,128)(2,1)} %bitcast.60), calls=%async_computation.1 | async-start | bytes 13107200 | tf_op jit(solution)/shard_map/all_to_all | solution.py:85
  288.6 17.0 %copy-start.5 = (f32[32,32]{1,0:T(8,128)S(1)}, f32[32,32]{1,0:T(8,128)}, u32[]{:S(2)}) copy-start(f32[32,32]{1,0:T(8,128)} %param.9) | copy-start | bytes 12292
  312.0 2.7 copy-start.1
  314.8 3.6 copy-start.3
  316.7 146.4 %collective-permute-start.1 = (bf16[80,32,640]{2,1,0:T(8,128)(2,1)}, bf16[80,32,640]{2,1,0:T(8,128)(2,1)}, u32[]{:S(2)}, u32[]{:S(2)}) collective-permute-start(bf16[80,32,640]{2,1,0:T(8,128)(2,1)} %constant_dynamic-slice_fusion), channel_id=1, source_target_pairs={{0,4},{4,0},{1,5},{5,1},{2,6},{6,2},{3,7},{7,3},{8,12},{12,8},{9,1... | collective-permute-start | bytes 9830408 | tf_op jit(solution)/shard_map/ppermute | solution.py:10
  493.7 21.3 %collective-permute-start.2 = (f32[80,2560]{1,0:T(8,128)S(1)}, f32[80,2560]{1,0:T(8,128)S(1)}, u32[]{:S(2)}, u32[]{:S(2)}) collective-permute-start(f32[80,2560]{1,0:T(8,128)S(1)} %broadcast_multiply_fusion), channel_id=1, source_target_pairs={{0,4},{4,0},{1,5},{5,1},{2,6},{6,2},{3,7},{7,3},{8,12},{12,8},{9,1... | collective-permute-start | bytes 2457608 | tf_op jit(solution)/shard_map/ppermute | solution.py:10

commit v2 on v1

--- a/solution.py
+++ b/solution.py
@@ -1,8 +1,11 @@
+import functools
 import math
 
 import jax
 import jax.numpy as jnp
 from jax import lax
+from jax.experimental import pallas as pl
+from jax.experimental.pallas import tpu as pltpu
 from jax.sharding import PartitionSpec as P
 
 
@@ -10,16 +13,154 @@
     return lax.ppermute(value, "member", [(0, 1), (1, 0)])
 
 
-def column_info(mw):
-    column = jnp.arange(2 * mw, dtype=jnp.int32)
+LANES = 128
+GROUP = 8
+
+
+def packs(n, width, levels, rows):
+    rest = width % LANES
+    return (
+        width // LANES == 1
+        and rest * n == LANES
+        and levels % n == 0
+        and levels % 16 == 0
+        and (rows // 2) % GROUP == 0
+    )
+
+
+def column_order(n, width, packed):
+    column = jnp.arange(n * width, dtype=jnp.int32)
+    if not packed:
+        return column
+    rest = width - LANES
+    tail = column - n * LANES
+    head = column // LANES * width + column % LANES
+    return jnp.where(tail < 0, head, tail // rest * width + LANES + tail % rest)
+
+
+def regroup(levels):
+    row = jnp.arange(GROUP * levels, dtype=jnp.int32)
+    source = row % GROUP * levels + row // GROUP
+    return (source[:, None] == row[None, :]).astype(jnp.bfloat16)
+
+
+def analysis_kernel(n, levels, scale, state_ref, table_ref, order_ref, out_ref):
+    rows = GROUP * levels
+    flat = state_ref[...].reshape(rows, state_ref.shape[2])
+    zonal = jnp.dot(flat, table_ref[...], preferred_element_type=jnp.float32)
+    zonal = (zonal * jnp.float32(scale)).astype(jnp.bfloat16)
+    zonal = jnp.dot(order_ref[...], zonal, preferred_element_type=jnp.float32)
+    for level in range(levels):
+        piece = zonal[level * GROUP : (level + 1) * GROUP]
+        for d in range(n):
+            out_ref[d, :, level * LANES : (level + 1) * LANES] = piece[
+                :, d * LANES : (d + 1) * LANES
+            ].astype(jnp.bfloat16)
+    rest = LANES // n
+    slot = lax.broadcasted_iota(jnp.int32, (GROUP, LANES), 1) // rest
+    for g in range(levels // n):
+        pieces = [
+            zonal[(n * g + q) * GROUP : (n * g + q + 1) * GROUP, n * LANES :] for q in range(n)
+        ]
+        for d in range(n):
+            total = pieces[d]
+            for q in range(n):
+                if q != d:
+                    moved = pltpu.roll(pieces[q], (q - d) % n * rest, 1)
+                    total = jnp.where(slot == q, moved, total)
+            at = (levels + g) * LANES
+            out_ref[d, :, at : at + LANES] = total.astype(jnp.bfloat16)
+
+
+def analysis(field, table, n):
+    rows, levels, nlon = field.shape
+    columns = table.shape[1]
+    lanes = levels * columns // n
+    order = regroup(levels)
+    scale = 1.0 / math.sqrt(nlon)
+    return pl.pallas_call(
+        functools.partial(analysis_kernel, n, levels, scale),
+        grid=(rows // GROUP,),
+        in_specs=[
+            pl.BlockSpec((GROUP, levels, nlon), lambda i: (i, 0, 0)),
+            pl.BlockSpec((nlon, columns), lambda i: (0, 0)),
+            pl.BlockSpec(order.shape, lambda i: (0, 0)),
+        ],
+        out_specs=pl.BlockSpec((n, GROUP, lanes), lambda i: (0, i, 0)),
+        out_shape=jax.ShapeDtypeStruct((n, rows, lanes), jnp.bfloat16),
+        cost_estimate=pl.CostEstimate(
+            flops=2 * rows * levels * nlon * columns,
+            bytes_accessed=2 * (field.size + n * rows * lanes),
+            transcendentals=0,
+        ),
+        name="analysis",
+    )(field, table, order)
+
+
+def mix_kernel(n, levels, packed_ref, high_ref, low_ref, out_ref, flat_ref):
+    rest = LANES // n
+    slot = lax.broadcasted_iota(jnp.int32, (GROUP, LANES), 1) // rest
+    for level in range(levels):
+        for d in range(n):
+            flat_ref[level * GROUP : (level + 1) * GROUP, d * LANES : (d + 1) * LANES] = packed_ref[
+                d, :, level * LANES : (level + 1) * LANES
+            ].astype(jnp.float32)
+    for g in range(levels // n):
+        at = (levels + g) * LANES
+        pieces = [packed_ref[d, :, at : at + LANES].astype(jnp.float32) for d in range(n)]
+        for q in range(n):
+            total = pieces[q]
+            for d in range(n):
+                if d != q:
+                    moved = pltpu.roll(pieces[d], (d - q) % n * rest, 1)
+                    total = jnp.where(slot == d, moved, total)
+            row = (n * g + q) * GROUP
+            flat_ref[row : row + GROUP, n * LANES :] = total
+    flat = flat_ref[...].astype(jnp.bfloat16)
+    mixed = jnp.dot(high_ref[...], flat, preferred_element_type=jnp.float32)
+    mixed += jnp.dot(low_ref[...], flat, preferred_element_type=jnp.float32)
+    out_ref[...] = mixed.astype(jnp.bfloat16).reshape(out_ref.shape)
+
+
+def mix(packed, weights):
+    n, rows, lanes = packed.shape
+    levels = weights.shape[0]
+    columns = n * lanes // levels
+    size = GROUP * levels
+    eye = jnp.eye(GROUP, dtype=jnp.float32)
+    full = weights[None, :, :, None] * eye[:, None, None, :]
+    full = full.reshape(size, size)
+    high = full.astype(jnp.bfloat16)
+    low = (full - high.astype(jnp.float32)).astype(jnp.bfloat16)
+    return pl.pallas_call(
+        functools.partial(mix_kernel, n, levels),
+        grid=(rows // GROUP,),
+        in_specs=[
+            pl.BlockSpec((n, GROUP, lanes), lambda i: (0, i, 0)),
+            pl.BlockSpec((size, size), lambda i: (0, 0)),
+            pl.BlockSpec((size, size), lambda i: (0, 0)),
+        ],
+        out_specs=pl.BlockSpec((GROUP, levels, columns), lambda i: (i, 0, 0)),
+        out_shape=jax.ShapeDtypeStruct((rows, levels, columns), jnp.bfloat16),
+        scratch_shapes=[pltpu.VMEM((size, columns), jnp.float32)],
+        cost_estimate=pl.CostEstimate(
+            flops=4 * rows * levels * size * columns,
+            bytes_accessed=4 * n * rows * lanes,
+            transcendentals=0,
+        ),
+        name="mix",
+    )(packed, high, low)
+
+
+def column_info(mw, column):
     part = column // mw
     rest = column % mw
     half = mw // 2
     return part, jnp.where(rest < half, 2 * rest + 2 * part, 2 * (rest - half) + 1)
 
 
-def lon_table(nlon, mw):
-    part, wave = column_info(mw)
+def lon_table(nlon, mw, column):
+    part, wave = column_info(mw, column)
     inner = math.gcd(nlon, 64)
     outer = nlon // inner
 
@@ -62,11 +203,15 @@
 
     other_state = swapped(lax.dynamic_slice_in_dim(field, theirs, half, 0))
 
-    table = lon_table(nlon, mw)
-    zonal = jnp.dot(field.reshape(rows * levels, nlon), table, preferred_element_type=f32)
-    zonal = (zonal * f32(1.0 / math.sqrt(nlon))).astype(bf16)
-    zonal = zonal.reshape(rows, levels, n, width).transpose(2, 0, 3, 1)
-    zonal = zonal.reshape(n, rows, width * levels)
+    packed = packs(n, width, levels, rows)
+    table = lon_table(nlon, mw, column_order(n, width, packed))
+    if packed:
+        zonal = analysis(field, table, n)
+    else:
+        zonal = jnp.dot(field.reshape(rows * levels, nlon), table, preferred_element_type=f32)
+        zonal = (zonal * f32(1.0 / math.sqrt(nlon))).astype(bf16)
+        zonal = zonal.reshape(rows, levels, n, width).transpose(2, 0, 1, 3)
+        zonal = zonal.reshape(n, rows, width * levels)
     gathered = lax.all_to_all(zonal, "lat", 0, 0, tiled=True).reshape(nlat, width * levels)
 
     odd = (lax.axis_index("lat") * width) % mw >= mw // 2
@@ -76,18 +221,37 @@
     spectral = jnp.dot(basis_hi, gathered, preferred_element_type=f32) + jnp.dot(
         basis_lo, gathered, preferred_element_type=f32
     )
-    gains = jnp.repeat(gain.T * f32(math.sqrt(2.0 / nlat)), levels, axis=1)
-    forcing = noise[0].reshape(width * levels, modes).T
+    cuts = ((0, LANES), (LANES, width)) if packed else ((0, width),)
+    scaled = gain.T * f32(math.sqrt(2.0 / nlat))
+    gains = jnp.concatenate([jnp.tile(scaled[:, a:b], (1, levels)) for a, b in cuts], axis=1)
+    forcing = jnp.concatenate(
+        [noise[0, a:b].transpose(2, 1, 0).reshape(modes, levels * (b - a)) for a, b in cuts], axis=1
+    )
     gains, forcing = lax.optimization_barrier((gains, forcing))
     forced = gains * spectral + forcing
     back = jnp.dot(basis.T, forced, precision=high) * f32(math.sqrt(2.0 / modes))
     back = back.astype(bf16).reshape(n, rows, width * levels)
-    returned = lax.all_to_all(back, "lat", 0, 0, tiled=True)
-    returned = returned.reshape(n, rows, width, levels).transpose(1, 3, 0, 2)
-    returned = returned.reshape(rows, levels, n * width)
-    mixed = jnp.einsum("ab,jbc->jac", vertical_mix * f32(1.0 / math.sqrt(mw)), returned.astype(f32), precision=high)
-    mixed = lax.optimization_barrier(mixed.astype(bf16))
-    other_mixed = swapped(lax.dynamic_slice_in_dim(mixed, theirs, half, 0))
+    weights = vertical_mix * f32(1.0 / math.sqrt(mw))
+
+    def exchange(start):
+        part = lax.dynamic_slice_in_dim(back, start, half, 1)
+        return lax.all_to_all(part, "lat", 0, 0, tiled=True)
+
+    def mixing(part):
+        if packed:
+            return mix(part, weights)
+        part = part.reshape(n, half, levels, width).transpose(1, 2, 0, 3)
+        part = part.reshape(half, levels, n * width).astype(f32)
+        return jnp.einsum("ab,jbc->jac", weights, part, precision=high).astype(bf16)
+
+    far_part = exchange(theirs)
+    other_part = swapped(far_part)
+    near_part = exchange(mine)
+    near_mixed, far_mixed = mixing(near_part), mixing(far_part)
+    first = jnp.where(me == 0, near_mixed, far_mixed)
+    second = jnp.where(me == 0, far_mixed, near_mixed)
+    mixed = lax.optimization_barrier(jnp.concatenate([first, second], axis=0))
+    other_mixed = mixing(other_part)
 
     def advance(start, coefficients):
         count = start.shape[0]

time: 527 us -> 478 us (0.907); the launches traced: 517 us -> 473 us
  local copies, waits for them, and re-layouts: 130 us -> 49.3 us
  Pallas kernels: 0 us -> 60 us
  waiting for transfers between devices: 225 us -> 176 us
  blocking collectives: 0 us -> 41.2 us
  matrix products: 104 us -> 72.7 us
  other arithmetic: 39.3 us -> 57.2 us
    pallas_call x0 -> x4, Pallas kernels: none -> 60 us  [the longest x1 33.3 us: analysis(): pl.pallas_call(functools.partial(analysis_kernel, n, levels, scale), grid...]
    all_to_all x1, waiting for transfers between devices: 72.4 us -> 21.7 us  [exchange(): return lax.all_to_all(part, 'lat', 0, 0, tiled=True)]
    reshape x3 -> x1, local copies, waits for them, and re-layouts: 43.9 us -> 1.57 us  [body(): noise[0, a:b].transpose(2, 1, 0).reshape(modes, levels * (b - a))]
    all_to_all x0 -> x1, blocking collectives: none -> 41.2 us  [exchange(): return lax.all_to_all(part, 'lat', 0, 0, tiled=True)]
    dot_general x2 -> x0, matrix products: 29.8 us -> none  [the longest x1 23.3 us: body(): jnp.dot(field.reshape(rows * levels, nlon), table, preferred_element_type...]
    ppermute x3, waiting for transfers between devices: 116 us -> 133 us  [swapped(): return lax.ppermute(value, 'member', [(0, 1), (1, 0)])]
    all_to_all x1, waiting for transfers between devices: 36.2 us -> 21 us  [body(): lax.all_to_all(zonal, 'lat', 0, 0, tiled=True).reshape(nlat, width * levels)]
    transpose x1 -> x4, local copies, waits for them, and re-layouts: 27.1 us -> 12.2 us  [body(): noise[0, a:b].transpose(2, 1, 0).reshape(modes, levels * (b - a))]
  transfers between devices with their start and end apart: 5 -> 5, of which waited for: 3 -> 3; matrix products, arithmetic and copies ran while one was open for 29% -> 29% of each run, Pallas kernels for 0% -> 6%
where the time goes in v2:
time: 478 us; the launch traced here: 473 us
  waiting for transfers between devices  176 us (37%)
  matrix products  72.7 us (15%)
  Pallas kernels  60 us (13%)
  other arithmetic  57.2 us (12%)
  local copies, waits for them, and re-layouts  49.3 us (10%)
  blocking collectives  41.2 us (9%)
  starting transfers between devices  15.8 us (3%)
    ppermute x3, waiting for transfers between devices, swapped(): return lax.ppermute(value, 'member', [(0, 1), (1, 0)])  133 us
    dot_general x2, matrix products, advance(): lax.dot_general(coefficients.reshape(count * levels, n * width), table, (...  46.2 us
    all_to_all x1, blocking collectives, exchange(): return lax.all_to_all(part, 'lat', 0, 0, tiled=True)  41.2 us
    pallas_call x1, Pallas kernels, analysis(): pl.pallas_call(functools.partial(analysis_kernel, n, levels, scale), grid...  33.3 us
    pallas_call x3, Pallas kernels, mix(): pl.pallas_call(functools.partial(mix_kernel, n, levels), grid=(rows // GR...  26.7 us
    all_to_all x1, waiting for transfers between devices, exchange(): return lax.all_to_all(part, 'lat', 0, 0, tiled=True)  21.7 us
    all_to_all x1, waiting for transfers between devices, body(): lax.all_to_all(zonal, 'lat', 0, 0, tiled=True).reshape(nlat, width * levels)  21 us
    reduce_sum x1, other arithmetic, body(): skill = jnp.mean(jnp.abs(updated.astype(f32) - target.astype(f32)), axis=1)  19.5 us
  transfers between devices with their start and end apart: 5, of which 3 were waited for; matrix products, arithmetic and copies ran while one was open for 29% of the time, Pallas kernels for 6%

profile of v2, /device:TPU:0, one launch (start us, length us, event | category | flops | bytes accessed | tf_op | source)
XLA Modules:
  0.0 473.3 jit_solution(991693314477531877)
XLA Ops:
  0.7 0.8 fusion.7.order_ref
  1.5 0.7 fusion.15
  2.1 0.5 negate_select_fusion
  2.7 2.7 add_convert_fusion
  5.4 33.3 %analysis.1 = bf16[4,160,5120]{2,1,0:T(8,128)(2,1)} custom-call(bf16[160,32,2560]{2,1,0:T(8,128)(2,1)} %bitcast.69, bf16[2560,640]{1,0:T(8,128)(2,1)} %bitcast.73, bf16[256,256]{1,0:T(8,128)(2,1)} %fusion.7.order_ref), custom_call_target="tpu_custom_call" | custom-call | flops 16777216000 | bytes 32768000 | tf_op jit(solution)/shard_map/analysis/pallas_call | solution.py:81
  38.6 5.8 %all-to-all-start = ((bf16[4,160,5120]{2,1,0:T(8,128)(2,1)}), bf16[4,160,5120]{2,1,0:T(8,128)(2,1)}, u32[]{:S(2)}, u32[]{:S(2)}) async-start(bf16[4,160,5120]{2,1,0:T(8,128)(2,1)} %analysis.1), calls=%async_computation | async-start | bytes 13107200 | tf_op jit(solution)/shard_map/all_to_all | solution.py:215
  44.5 10.8 %dynamic-slice_bitcast_fusion = bf16[80,32,2560]{2,1,0:T(8,128)(2,1)} fusion(bf16[1,160,32,2560]{3,2,1,0:T(8,128)(2,1)} %param.5, s32[]{:T(128)S(6)} %select_n.242), kind=kLoop, calls=%fused_computation.8 | loop fusion | bytes 26214404 | tf_op jit(solution)/shard_map/dynamic_slice | solution.py:204
  55.3 3.1 collective-permute-start
  58.6 2.9 fusion.6
  61.5 0.2 tile.20
  61.7 1.5 copy.10
  63.2 1.5 slice_bitcast_fusion.1
  64.7 0.9 copy.12
  65.7 1.6 copy.13
  67.2 0.3 tile.8
  67.6 7.3 %copy.22 = f32[40,8,32,128]{3,1,2,0:T(8,128)} copy(f32[40,8,32,128]{3,2,1,0:T(8,128)S(1)} %bitcast.59) | data formatting | bytes 10485760
  74.9 3.2 slice_bitcast_fusion
  78.1 6.6 %copy.11 = f32[320,32,128]{2,1,0:T(8,128)} copy(f32[320,32,128]{0,1,2:T(8,128)} %slice_bitcast_fusion) | data formatting | bytes 10485760 | tf_op jit(solution)/shard_map/transpose | solution.py:228
  84.7 7.6 %copy.21 = f32[40,8,32,128]{3,1,2,0:T(8,128)S(1)} copy(f32[40,8,32,128]{3,2,1,0:T(8,128)} %bitcast.60) | data formatting | bytes 10485760
  92.4 5.3 %pad_maximum_fusion = (f32[320,5120]{1,0:T(8,128)}, f32[320,5120]{1,0:T(8,128)}) fusion(f32[320,1024]{1,0:T(8,128)S(1)} %copy-done.4, f32[320,4096]{1,0:T(8,128)S(1)} %bitcast.63, f32[320,1024]{1,0:T(8,128)S(1)} %copy-done.5, f32[320,4096]{1,0:T(8,128)S(1)} %bitcast.64), kind=kLoop, calls=%fused_computation.13 | loop fusion | flops 3276800 | bytes 26214400 | tf_op jit(solution)/shard_map/concatenate | solution.py:226
  97.7 21.0 %all-to-all-done = bf16[4,160,5120]{2,1,0:T(8,128)(2,1)} async-done(((bf16[4,160,5120]{2,1,0:T(8,128)(2,1)}), bf16[4,160,5120]{2,1,0:T(8,128)(2,1)}, u32[]{:S(2)}, u32[]{:S(2)}) %all-to-all-start) | async-done | bytes 6553632 | tf_op jit(solution)/shard_map/all_to_all | solution.py:215
  118.7 7.8 %fusion.9 = f32[320,5120]{1,0:T(8,128)} fusion(bf16[640,5120]{1,0:T(8,128)(2,1)} %bitcast.10, f32[320,640]{1,0:T(8,128)S(1)} %fusion.6), kind=kOutput, calls=%fused_computation.38 | convolution fusion | flops 2097356800 | bytes 13926400 | tf_op jit(solution)/shard_map/dot_general | solution.py:221
  126.5 1.2 copy-done.1
  127.7 7.6 %fusion.5 = f32[320,5120]{1,0:T(8,128)S(1)} fusion(f32[320,5120]{1,0:T(8,128)S(1)} %copy-done.1, f32[320,5120]{1,0:T(8,128)S(1)} %copy-done, f32[320,5120]{1,0:T(8,128)} %fusion.9, bf16[640,5120]{1,0:T(8,128)(2,1)} %bitcast.10, f32[320,640]{1,0:T(8,128)S(1)} %fusion.6), kind=kOutput, calls=%fused_computation.12 | convolution fusion | flops 2102886400 | bytes 33587200 | tf_op jit(solution)/shard_map/dot_general | solution.py:221
  135.3 11.2 %multiply_convert_fusion = bf16[640,5120]{1,0:T(8,128)(2,1)S(1)} fusion(f32[320,640]{1,0:T(8,128)S(1)} %fusion.6, f32[320,5120]{1,0:T(8,128)S(1)} %fusion.5), kind=kOutput, calls=%fused_computation.9 | convolution fusion | flops 6298009600 | bytes 13926400 | tf_op jit(solution)/shard_map/dot_general | solution.py:232
  146.5 2.3 constant_dynamic-slice_fusion.1
  148.7 41.2 %all_to_all.15.packed_ref = bf16[4,80,5120]{2,1,0:T(8,128)(2,1)} all-to-all(bf16[4,80,5120]{2,1,0:T(8,128)(2,1)S(1)} %get-tuple-element.18), channel_id=1, replica_groups=mesh['ic'=4,'member'=2,'lat'=4] {'lat'}, dimensions={0} | all-to-all | bytes 6553600 | tf_op jit(solution)/shard_map/all_to_all | solution.py:238
  189.9 3.9 all-to-all-start.2
  193.9 1.2 broadcast_multiply_fusion
  195.1 1.5 mul.296
  196.6 0.8 copy.15
  197.5 1.8 subtract_convert_fusion.2
  199.2 8.9 %mix.3 = bf16[80,32,640]{2,1,0:T(8,128)(2,1)} custom-call(bf16[4,80,5120]{2,1,0:T(8,128)(2,1)} %all_to_all.15.packed_ref, bf16[256,256]{1,0:T(8,128)(2,1)} %get-tuple-element.15.high_ref, bf16[256,256]{1,0:T(8,128)(2,1)} %get-tuple-element.14.low_ref), custom_call_target="tpu_custom_call" | custom-call | flops 1677721600 | bytes 6553600 | tf_op jit(solution)/shard_map/mix/pallas_call | solution.py:135
  208.1 21.7 %all-to-all-done.2.packed_ref = bf16[4,80,5120]{2,1,0:T(8,128)(2,1)S(1)} async-done(((bf16[4,80,5120]{2,1,0:T(8,128)(2,1)}), bf16[4,80,5120]{2,1,0:T(8,128)(2,1)S(1)}, u32[]{:S(2)}, u32[]{:S(2)}) %all-to-all-start.2) | async-done | bytes 3276832 | tf_op jit(solution)/shard_map/all_to_all | solution.py:238
  229.8 1.7 copy-done.2
  231.5 8.8 %mix.4 = bf16[80,32,640]{2,1,0:T(8,128)(2,1)} custom-call(bf16[4,80,5120]{2,1,0:T(8,128)(2,1)} %copy-done.2, bf16[256,256]{1,0:T(8,128)(2,1)} %get-tuple-element.15.high_ref, bf16[256,256]{1,0:T(8,128)(2,1)} %get-tuple-element.14.low_ref), custom_call_target="tpu_custom_call" | custom-call | flops 1677721600 | bytes 6553600 | tf_op jit(solution)/shard_map/mix/pallas_call | solution.py:135
  240.3 3.5 broadcast_select_fusion.1
  243.9 3.4 pad_maximum_fusion.2
  247.2 1.3 collective-permute-start.1
  248.5 28.8 %fusion = bf16[5120,2560]{1,0:T(8,128)(2,1)} fusion(bf16[5120,2560]{1,0:T(8,128)(2,1)} %bitcast.70, bf16[5120,640]{1,0:T(8,128)(2,1)} %bitcast.68, bf16[2560,640]{1,0:T(8,128)(2,1)} %bitcast.74), kind=kOutput, calls=%fused_computation.1 | convolution fusion | flops 16816537600 | bytes 62259200 | tf_op jit(solution)/shard_map/dot_general | solution.py:258
  277.3 133.2 %collective-permute-done.1.packed_ref = bf16[4,80,5120]{2,1,0:T(8,128)(2,1)} collective-permute-done((bf16[4,80,5120]{2,1,0:T(8,128)(2,1)S(1)}, bf16[4,80,5120]{2,1,0:T(8,128)(2,1)}, u32[]{:S(2)}, u32[]{:S(2)}) %collective-permute-start.1) | collective-permute-done | bytes 3276832 | tf_op jit(solution)/shard_map/ppermute | solution.py:13
  410.5 9.0 %mix.5 = bf16[80,32,640]{2,1,0:T(8,128)(2,1)} custom-call(bf16[4,80,5120]{2,1,0:T(8,128)(2,1)} %collective-permute-done.1.packed_ref, bf16[256,256]{1,0:T(8,128)(2,1)} %get-tuple-element.15.high_ref, bf16[256,256]{1,0:T(8,128)(2,1)} %get-tuple-element.14.low_ref), custom_call_target="tpu_custom_call" | custom-call | flops 1677721600 | bytes 6553600 | tf_op jit(solution)/shard_map/mix/pallas_call | solution.py:135
  419.5 17.4 %fusion.3 = bf16[2560,2560]{1,0:T(8,128)(2,1)} fusion(bf16[80,32,2560]{2,1,0:T(8,128)(2,1)} %collective-permute-done, bf16[2560,640]{1,0:T(8,128)(2,1)} %bitcast.76, bf16[2560,640]{1,0:T(8,128)(2,1)S(1)} %bitcast.75), kind=kOutput, calls=%fused_computation.7 | convolution fusion | flops 8408268800 | bytes 32768000 | tf_op jit(solution)/shard_map/dot_general | solution.py:258
  436.9 13.2 %fusion.2 = f32[80,2560]{1,0:T(8,128)S(1)} fusion(bf16[80,32,2560]{2,1,0:T(8,128)(2,1)} %bitcast.65, bf16[160,32,2560]{2,1,0:T(8,128)(2,1)} %bitcast.55, s32[]{:T(128)S(6)} %select_n.241), kind=kLoop, calls=%fused_computation.5 | loop fusion | flops 32563200 | bytes 27033604 | tf_op jit(solution)/shard_map/reduce_sum | solution.py:271
  450.1 1.8 collective-permute-start.2
  451.9 19.5 %abs_reduce_fusion = f32[160,2560]{1,0:T(8,128)S(1)} fusion(bf16[160,32,2560]{2,1,0:T(8,128)(2,1)} %param.6, bf16[160,32,2560]{2,1,0:T(8,128)(2,1)} %bitcast.56), kind=kLoop, calls=%fused_computation.2 | loop fusion | flops 65126400 | bytes 54067200 | tf_op jit(solution)/shard_map/reduce_sum | solution.py:268
  471.5 0.2 select_bitcast_fusion.1
  471.6 1.4 maximum_subtract_fusion
  (42 shorter events, 0.4 us)
Async XLA Ops:
  38.6 80.0 %all-to-all-start = ((bf16[4,160,5120]{2,1,0:T(8,128)(2,1)}), bf16[4,160,5120]{2,1,0:T(8,128)(2,1)}, u32[]{:S(2)}, u32[]{:S(2)}) async-start(bf16[4,160,5120]{2,1,0:T(8,128)(2,1)} %analysis.1), calls=%async_computation | async-start | bytes 13107200 | tf_op jit(solution)/shard_map/all_to_all | solution.py:215
  44.5 13.9 %copy-start.7 = (f32[160,320]{1,0:T(8,128)S(1)}, f32[160,320]{1,0:T(8,128)}, u32[]{:S(2)}) copy-start(f32[160,320]{1,0:T(8,128)} %param.8) | copy-start | bytes 614404
  55.3 364.2 %collective-permute-start = (bf16[80,32,2560]{2,1,0:T(8,128)(2,1)}, bf16[80,32,2560]{2,1,0:T(8,128)(2,1)}, u32[]{:S(2)}, u32[]{:S(2)}) collective-permute-start(bf16[80,32,2560]{2,1,0:T(8,128)(2,1)} %dynamic-slice_bitcast_fusion), channel_id=1, source_target_pairs={{0,4},{4,0},{1,5},{5,1},{2,6},{6,2},{3,7},{7,3},{8,12},{12,8},{9,1... | collective-permute-start | bytes 39321608 | tf_op jit(solution)/shard_map/ppermute | solution.py:13
  67.2 7.6 %slice-start.2 = ((s8[7864320]{0:T(1024)(128)(4,1)}), s8[4194304]{0:T(1024)(128)(4,1)S(1)}, s32[]{:S(2)}) async-start(s8[7864320]{0:T(1024)(128)(4,1)} %bitcast.66), calls=%async_computation.5 | async-start | bytes 8388608
  67.6 7.3 %slice-start.3 = ((s8[7864320]{0:T(1024)(128)(4,1)}), s8[3670016]{0:T(1024)(128)(4,1)S(1)}, s32[]{:S(2)}) async-start(s8[7864320]{0:T(1024)(128)(4,1)} %bitcast.66), calls=%async_computation.6 | async-start | bytes 7340032
  84.7 7.6 %slice-start = ((s8[5242880]{0:T(1024)(128)(4,1)}), s8[4194304]{0:T(1024)(128)(4,1)S(1)}, s32[]{:S(2)}) async-start(s8[5242880]{0:T(1024)(128)(4,1)} %bitcast.61), calls=%async_computation.3 | async-start | bytes 8388608
  84.7 7.6 %copy-start.4 = (f32[320,1024]{1,0:T(8,128)S(1)}, f32[320,1024]{1,0:T(8,128)}, u32[]{:S(2)}) copy-start(f32[320,1024]{1,0:T(8,128)} %copy.10) | copy-start | bytes 3932164
  84.7 7.6 %copy-start.5 = (f32[320,1024]{1,0:T(8,128)S(1)}, f32[320,1024]{1,0:T(8,128)}, u32[]{:S(2)}) copy-start(f32[320,1024]{1,0:T(8,128)} %copy.13) | copy-start | bytes 3932164
  84.7 7.6 %slice-start.1 = ((s8[5242880]{0:T(1024)(128)(4,1)}), s8[1048576]{0:T(1024)(128)(4,1)S(1)}, s32[]{:S(2)}) async-start(s8[5242880]{0:T(1024)(128)(4,1)} %bitcast.61), calls=%async_computation.4 | async-start | bytes 2097152
  118.7 7.8 %copy-start = (f32[320,5120]{1,0:T(8,128)S(1)}, f32[320,5120]{1,0:T(8,128)}, u32[]{:S(2)}) copy-start(f32[320,5120]{1,0:T(8,128)} %get-tuple-element.8) | copy-start | bytes 19660804
  118.7 9.0 %copy-start.1 = (f32[320,5120]{1,0:T(8,128)S(1)}, f32[320,5120]{1,0:T(8,128)}, u32[]{:S(2)}) copy-start(f32[320,5120]{1,0:T(8,128)} %get-tuple-element.13) | copy-start | bytes 19660804
  148.7 45.1 %copy-start.8 = (f32[32,32]{1,0:T(8,128)S(1)}, f32[32,32]{1,0:T(8,128)}, u32[]{:S(2)}) copy-start(f32[32,32]{1,0:T(8,128)} %param.9) | copy-start | bytes 12292
  189.9 39.9 %all-to-all-start.2 = ((bf16[4,80,5120]{2,1,0:T(8,128)(2,1)}), bf16[4,80,5120]{2,1,0:T(8,128)(2,1)S(1)}, u32[]{:S(2)}, u32[]{:S(2)}) async-start(bf16[4,80,5120]{2,1,0:T(8,128)(2,1)} %get-tuple-element.19), calls=%async_computation.2 | async-start | bytes 6553600 | tf_op jit(solution)/shard_map/all_to_all | solution.py:238
  229.8 1.7 copy-start.2
  243.8 3.4 copy-start.3
  247.2 163.2 %collective-permute-start.1 = (bf16[4,80,5120]{2,1,0:T(8,128)(2,1)S(1)}, bf16[4,80,5120]{2,1,0:T(8,128)(2,1)}, u32[]{:S(2)}, u32[]{:S(2)}) collective-permute-start(bf16[4,80,5120]{2,1,0:T(8,128)(2,1)S(1)} %copy-done.3), channel_id=1, source_target_pairs={{0,4},{4,0},{1,5},{5,1},{2,6},{6,2},{3,7},{7,3},{8,12},{12,8},{9,1... | collective-permute-start | bytes 9830408 | tf_op jit(solution)/shard_map/ppermute | solution.py:13
  410.5 9.0 %copy-start.6 = (bf16[40,64,640]{2,1,0:T(8,128)(2,1)S(1)}, bf16[40,64,640]{2,1,0:T(8,128)(2,1)}, u32[]{:S(2)}) copy-start(bf16[40,64,640]{2,1,0:T(8,128)(2,1)} %add_convert_fusion) | copy-start | bytes 9830404
  450.1 21.3 %collective-permute-start.2 = (f32[80,2560]{1,0:T(8,128)S(1)}, f32[80,2560]{1,0:T(8,128)S(1)}, u32[]{:S(2)}, u32[]{:S(2)}) collective-permute-start(f32[80,2560]{1,0:T(8,128)S(1)} %broadcast_multiply_fusion.1), channel_id=1, source_target_pairs={{0,4},{4,0},{1,5},{5,1},{2,6},{6,2},{3,7},{7,3},{8,12},{12,8},{9,1... | collective-permute-start | bytes 2457608 | tf_op jit(solution)/shard_map/ppermute | solution.py:13

commit v3 on v2

--- a/solution.py
+++ b/solution.py
@@ -201,7 +201,15 @@
     me = lax.axis_index("member")
     mine, theirs = me * half, (1 - me) * half
 
-    other_state = swapped(lax.dynamic_slice_in_dim(field, theirs, half, 0))
+    quarter = half // 4
+    cut = 3 * quarter
+
+    def send(start, count):
+        return swapped(lax.dynamic_slice_in_dim(field, theirs + start, count, 0))
+
+    head_a = send(0, quarter)
+    head_b = send(quarter, cut - quarter)
+    tail = send(cut, half - cut)
 
     packed = packs(n, width, levels, rows)
     table = lon_table(nlon, mw, column_order(n, width, packed))
@@ -266,10 +274,19 @@
 
     updated = advance(field, mixed)
     skill = jnp.mean(jnp.abs(updated.astype(f32) - target.astype(f32)), axis=1)
-    other = advance(other_state, other_mixed)
-    own = lax.dynamic_slice_in_dim(updated, mine, half, 0)
-    spread = 0.5 * jnp.mean(jnp.abs(own.astype(f32) - other.astype(f32)), axis=1)
-    far = swapped(spread)
+    skill = lax.optimization_barrier(skill)
+
+    def spread_of(other_rows, start):
+        count = other_rows.shape[0]
+        other = advance(other_rows, lax.slice_in_dim(other_mixed, start, start + count, axis=0))
+        own = lax.dynamic_slice_in_dim(updated, mine + start, count, 0)
+        return 0.5 * jnp.mean(jnp.abs(own.astype(f32) - other.astype(f32)), axis=1)
+
+    head = jnp.concatenate([spread_of(head_a, 0), spread_of(head_b, quarter)], axis=0)
+    head, tail = lax.optimization_barrier((head, tail))
+    last = spread_of(tail, cut)
+    far = jnp.concatenate([swapped(head), swapped(last)], axis=0)
+    spread = jnp.concatenate([head, last], axis=0)
     first = jnp.where(me == 0, spread, far)
     second = jnp.where(me == 0, far, spread)
     crps = skill - jnp.concatenate([first, second], axis=0)

time: 478 us -> 618 us (1.29)
  waiting for transfers between devices: 176 us -> 304 us
  local copies, waits for them, and re-layouts: 49.3 us -> 57.4 us
    ppermute x3 -> x6, waiting for transfers between devices: 133 us -> 271 us  [swapped(): return lax.ppermute(value, 'member', [(0, 1), (1, 0)])]
    all_to_all x1, waiting for transfers between devices: 21.7 us -> 5.26 us  [exchange(): return lax.all_to_all(part, 'lat', 0, 0, tiled=True)]
    unnamed x28 -> x18, local copies, waits for them, and re-layouts: 17.8 us -> 19.8 us
    dynamic_slice x1 -> x2, local copies, waits for them, and re-layouts: 10.8 us -> 12.7 us  [send(): return swapped(lax.dynamic_slice_in_dim(field, theirs + start, count, 0))]
    dot_general x2 -> x4, matrix products: 46.2 us -> 45.4 us  [advance(): lax.dot_general(coefficients.reshape(count * levels, n * width), table, (...]
    reduce_sum x1 -> x3, other arithmetic: 13.2 us -> 13.1 us  [spread_of(): return 0.5 * jnp.mean(jnp.abs(own.astype(f32) - other.astype(f32)), axis=1)]
  transfers between devices with their start and end apart: 5 -> 8, of which waited for: 3 -> 5; matrix products, arithmetic and copies ran while one was open for 29% -> 24% of each run, Pallas kernels for 6% -> 4%
where the time goes in v3:
time: 618 us; the launch traced here: 614 us
  waiting for transfers between devices  304 us (49%)
  matrix products  72 us (12%)
  other arithmetic  61.7 us (10%)
  Pallas kernels  60 us (10%)
  local copies, waits for them, and re-layouts  57.4 us (9%)
  blocking collectives  41.1 us (7%)
  starting transfers between devices  17.1 us (3%)
    ppermute x6, waiting for transfers between devices, swapped(): return lax.ppermute(value, 'member', [(0, 1), (1, 0)])  271 us
    dot_general x4, matrix products, advance(): lax.dot_general(coefficients.reshape(count * levels, n * width), table, (...  45.4 us
    all_to_all x1, blocking collectives, exchange(): return lax.all_to_all(part, 'lat', 0, 0, tiled=True)  41.1 us
    pallas_call x1, Pallas kernels, analysis(): pl.pallas_call(functools.partial(analysis_kernel, n, levels, scale), grid...  33.3 us
    all_to_all x1, waiting for transfers between devices, body(): lax.all_to_all(zonal, 'lat', 0, 0, tiled=True).reshape(nlat, width * levels)  27 us
    pallas_call x3, Pallas kernels, mix(): pl.pallas_call(functools.partial(mix_kernel, n, levels), grid=(rows // GR...  26.7 us
    reduce_sum x1, other arithmetic, body(): skill = jnp.mean(jnp.abs(updated.astype(f32) - target.astype(f32)), axis=1)  20.7 us
    unnamed x18, local copies, waits for them, and re-layouts  19.8 us
  transfers between devices with their start and end apart: 8, of which 5 were waited for; matrix products, arithmetic and copies ran while one was open for 24% of the time, Pallas kernels for 4%

profile of v3, /device:TPU:0, one launch (start us, length us, event | category | flops | bytes accessed | tf_op | source)
XLA Modules:
  0.0 613.9 jit_solution(11962599029566141009)
XLA Ops:
  1.9 2.7 add_convert_fusion
  5.4 33.3 %analysis.1 = bf16[4,160,5120]{2,1,0:T(8,128)(2,1)} custom-call(bf16[160,32,2560]{2,1,0:T(8,128)(2,1)} %bitcast.82, bf16[2560,640]{1,0:T(8,128)(2,1)} %bitcast.90, bf16[256,256]{1,0:T(8,128)(2,1)} %fusion.16.order_ref), custom_call_target="tpu_custom_call" | custom-call | flops 16777216000 | bytes 32768000 | tf_op jit(solution)/shard_map/analysis/pallas_call | solution.py:81
  38.7 6.0 all-to-all-start
  44.8 2.9 fusion.13
  48.2 7.1 %copy.22 = f32[40,8,32,128]{3,1,2,0:T(8,128)} copy(f32[40,8,32,128]{3,2,1,0:T(8,128)S(1)} %bitcast.77) | data formatting | bytes 10485760
  55.5 1.5 copy.10
  57.0 6.0 slice_bitcast_fusion
  63.0 6.5 %copy.11 = f32[320,32,128]{2,1,0:T(8,128)} copy(f32[320,32,128]{0,1,2:T(8,128)} %slice_bitcast_fusion) | data formatting | bytes 10485760 | tf_op jit(solution)/shard_map/transpose | solution.py:236
  69.6 9.7 %copy.21 = f32[40,8,32,128]{3,1,2,0:T(8,128)} copy(f32[40,8,32,128]{3,2,1,0:T(8,128)} %bitcast.78) | data formatting | bytes 10485760
  79.3 1.5 slice_bitcast_fusion.1
  81.7 1.5 copy.13
  83.3 8.5 %pad_maximum_fusion = (f32[320,5120]{1,0:T(8,128)}, f32[320,5120]{1,0:T(8,128)}) fusion(f32[320,1024]{1,0:T(8,128)} %copy.10, f32[320,4096]{1,0:T(8,128)} %bitcast.79, f32[320,1024]{1,0:T(8,128)} %copy.13, f32[320,4096]{1,0:T(8,128)} %bitcast.80), kind=kLoop, calls=%fused_computation.12 | loop fusion | flops 3276800 | bytes 26214400 | tf_op jit(solution)/shard_map/concatenate | solution.py:234
  91.8 27.0 %all-to-all-done = bf16[4,160,5120]{2,1,0:T(8,128)(2,1)} async-done(((bf16[4,160,5120]{2,1,0:T(8,128)(2,1)}), bf16[4,160,5120]{2,1,0:T(8,128)(2,1)}, u32[]{:S(2)}, u32[]{:S(2)}) %all-to-all-start) | async-done | bytes 6553632 | tf_op jit(solution)/shard_map/all_to_all | solution.py:223
  118.8 7.8 %fusion.18 = f32[320,5120]{1,0:T(8,128)} fusion(bf16[640,5120]{1,0:T(8,128)(2,1)} %bitcast.10, f32[320,640]{1,0:T(8,128)S(1)} %fusion.13), kind=kOutput, calls=%fused_computation.55 | convolution fusion | flops 2097356800 | bytes 13926400 | tf_op jit(solution)/shard_map/dot_general | solution.py:229
  126.7 1.2 copy-done.1
  127.8 7.6 %fusion.5 = f32[320,5120]{1,0:T(8,128)S(1)} fusion(f32[320,5120]{1,0:T(8,128)S(1)} %copy-done.1, f32[320,5120]{1,0:T(8,128)S(1)} %copy-done, f32[320,5120]{1,0:T(8,128)} %fusion.18, bf16[640,5120]{1,0:T(8,128)(2,1)} %bitcast.10, f32[320,640]{1,0:T(8,128)S(1)} %fusion.13), kind=kOutput, calls=%fused_computation.11 | convolution fusion | flops 2102886400 | bytes 33587200 | tf_op jit(solution)/shard_map/dot_general | solution.py:229
  135.4 11.2 %multiply_convert_fusion = bf16[640,5120]{1,0:T(8,128)(2,1)S(1)} fusion(f32[320,640]{1,0:T(8,128)S(1)} %fusion.13, f32[320,5120]{1,0:T(8,128)S(1)} %fusion.5), kind=kOutput, calls=%fused_computation.8 | convolution fusion | flops 6298009600 | bytes 13926400 | tf_op jit(solution)/shard_map/dot_general | solution.py:240
  146.6 2.2 constant_dynamic-slice_fusion.1
  148.8 41.1 %all_to_all.15.packed_ref = bf16[4,80,5120]{2,1,0:T(8,128)(2,1)} all-to-all(bf16[4,80,5120]{2,1,0:T(8,128)(2,1)S(1)} %get-tuple-element.25), channel_id=1, replica_groups=mesh['ic'=4,'member'=2,'lat'=4] {'lat'}, dimensions={0} | all-to-all | bytes 6553600 | tf_op jit(solution)/shard_map/all_to_all | solution.py:246
  189.9 4.1 all-to-all-start.1
  194.1 6.4 %dynamic-slice_bitcast_fusion.1 = (bf16[20,32,2560]{2,1,0:T(8,128)(2,1)}, bf16[20,32,2560]{2,1,0:T(8,128)(2,1)}) fusion(bf16[1,160,32,2560]{3,2,1,0:T(8,128)(2,1)} %param.5, s32[]{:T(128)S(6)} %select_n.260, s32[]{:T(128)S(6)} %select_n.254), kind=kLoop, calls=%fused_computation.30 | loop fusion | bytes 13107208 | tf_op jit(solution)/shard_map/dynamic_slice | solution.py:208
  200.4 1.6 collective-permute-start
  202.1 6.4 %dynamic-slice_bitcast_fusion = bf16[40,32,2560]{2,1,0:T(8,128)(2,1)} fusion(bf16[1,160,32,2560]{3,2,1,0:T(8,128)(2,1)} %param.5, s32[]{:T(128)S(6)} %select_n.259), kind=kLoop, calls=%fused_computation.25 | loop fusion | bytes 13107204 | tf_op jit(solution)/shard_map/dynamic_slice | solution.py:208
  208.8 1.6 collective-permute-start.3
  211.7 1.5 mul.304
  214.1 1.8 subtract_convert_fusion.2
  215.9 8.8 %mix.4 = bf16[80,32,640]{2,1,0:T(8,128)(2,1)} custom-call(bf16[4,80,5120]{2,1,0:T(8,128)(2,1)} %all_to_all.15.packed_ref, bf16[256,256]{1,0:T(8,128)(2,1)} %get-tuple-element.19.high_ref, bf16[256,256]{1,0:T(8,128)(2,1)} %get-tuple-element.18.low_ref), custom_call_target="tpu_custom_call" | custom-call | flops 1677721600 | bytes 6553600 | tf_op jit(solution)/shard_map/mix/pallas_call | solution.py:135
  224.7 5.3 all-to-all-done.1.packed_ref
  230.0 1.7 copy-done.3
  231.7 8.8 %mix.3 = bf16[80,32,640]{2,1,0:T(8,128)(2,1)} custom-call(bf16[4,80,5120]{2,1,0:T(8,128)(2,1)} %copy-done.3, bf16[256,256]{1,0:T(8,128)(2,1)} %get-tuple-element.19.high_ref, bf16[256,256]{1,0:T(8,128)(2,1)} %get-tuple-element.18.low_ref), custom_call_target="tpu_custom_call" | custom-call | flops 1677721600 | bytes 6553600 | tf_op jit(solution)/shard_map/mix/pallas_call | solution.py:135
  240.5 3.5 broadcast_select_fusion.1
  244.1 3.4 pad_maximum_fusion.2
  247.4 1.3 collective-permute-start.1
  248.7 28.8 %fusion = bf16[5120,2560]{1,0:T(8,128)(2,1)} fusion(bf16[5120,2560]{1,0:T(8,128)(2,1)} %bitcast.83, bf16[5120,640]{1,0:T(8,128)(2,1)} %bitcast.84, bf16[2560,640]{1,0:T(8,128)(2,1)} %bitcast.91), kind=kOutput, calls=%fused_computation.1 | convolution fusion | flops 16816537600 | bytes 62259200 | tf_op jit(solution)/shard_map/dot_general | solution.py:266
  277.5 20.7 %abs_reduce_fusion = f32[160,2560]{1,0:T(8,128)} fusion(bf16[160,32,2560]{2,1,0:T(8,128)(2,1)} %param.6, bf16[160,32,2560]{2,1,0:T(8,128)(2,1)} %bitcast.71), kind=kLoop, calls=%fused_computation.2 | loop fusion | flops 65126400 | bytes 54067200 | tf_op jit(solution)/shard_map/reduce_sum | solution.py:276
  298.2 254.3 %collective-permute-done.1.packed_ref = bf16[4,80,5120]{2,1,0:T(8,128)(2,1)} collective-permute-done((bf16[4,80,5120]{2,1,0:T(8,128)(2,1)S(1)}, bf16[4,80,5120]{2,1,0:T(8,128)(2,1)}, u32[]{:S(2)}, u32[]{:S(2)}) %collective-permute-start.1) | collective-permute-done | bytes 3276832 | tf_op jit(solution)/shard_map/ppermute | solution.py:13
  552.5 9.0 %mix.5 = bf16[80,32,640]{2,1,0:T(8,128)(2,1)} custom-call(bf16[4,80,5120]{2,1,0:T(8,128)(2,1)} %collective-permute-done.1.packed_ref, bf16[256,256]{1,0:T(8,128)(2,1)} %get-tuple-element.19.high_ref, bf16[256,256]{1,0:T(8,128)(2,1)} %get-tuple-element.18.low_ref), custom_call_target="tpu_custom_call" | custom-call | flops 1677721600 | bytes 6553600 | tf_op jit(solution)/shard_map/mix/pallas_call | solution.py:135
  561.5 1.5 fusion.62
  563.0 4.6 fusion.11
  567.6 3.5 fusion.10
  571.2 7.6 %fusion.3 = bf16[1280,2560]{1,0:T(8,128)(2,1)S(1)} fusion(bf16[40,32,2560]{2,1,0:T(8,128)(2,1)} %collective-permute-done.2, bf16[1280,640]{1,0:T(8,128)(2,1)S(1)} %bitcast.81, bf16[2560,640]{1,0:T(8,128)(2,1)S(1)} %bitcast.93), kind=kOutput, calls=%fused_computation.7 | convolution fusion | flops 4204134400 | bytes 18022400 | tf_op jit(solution)/shard_map/dot_general | solution.py:266
  578.8 6.1 fusion.2
  585.0 4.4 fusion.8
  589.5 3.5 fusion.7
  593.0 1.3 collective-permute-start.5
  595.2 6.7 %collective-permute-done.5 = f32[20,2560]{1,0:T(8,128)S(1)} collective-permute-done((f32[20,2560]{1,0:T(8,128)S(1)}, f32[20,2560]{1,0:T(8,128)S(1)}, u32[]{:S(2)}, u32[]{:S(2)}) %collective-permute-start.5) | collective-permute-done | bytes 204832 | tf_op jit(solution)/shard_map/ppermute | solution.py:13
  601.9 10.3 %collective-permute-done.4 = f32[60,2560]{1,0:T(8,128)S(1)} collective-permute-done((f32[60,2560]{1,0:T(8,128)S(1)}, f32[60,2560]{1,0:T(8,128)S(1)}, u32[]{:S(2)}, u32[]{:S(2)}) %collective-permute-start.4) | collective-permute-done | bytes 614432 | tf_op jit(solution)/shard_map/ppermute | solution.py:13
  612.3 1.3 fusion.12
  (48 shorter events, 7.3 us)
Async XLA Ops:
  38.7 6.0 copy-start.6
  38.7 80.2 %all-to-all-start = ((bf16[4,160,5120]{2,1,0:T(8,128)(2,1)}), bf16[4,160,5120]{2,1,0:T(8,128)(2,1)}, u32[]{:S(2)}, u32[]{:S(2)}) async-start(bf16[4,160,5120]{2,1,0:T(8,128)(2,1)} %analysis.1), calls=%async_computation | async-start | bytes 13107200 | tf_op jit(solution)/shard_map/all_to_all | solution.py:223
  118.8 7.8 %copy-start = (f32[320,5120]{1,0:T(8,128)S(1)}, f32[320,5120]{1,0:T(8,128)}, u32[]{:S(2)}) copy-start(f32[320,5120]{1,0:T(8,128)} %get-tuple-element.10) | copy-start | bytes 19660804
  118.8 9.0 %copy-start.1 = (f32[320,5120]{1,0:T(8,128)S(1)}, f32[320,5120]{1,0:T(8,128)}, u32[]{:S(2)}) copy-start(f32[320,5120]{1,0:T(8,128)} %get-tuple-element.15) | copy-start | bytes 19660804
  189.9 40.1 %all-to-all-start.1 = ((bf16[4,80,5120]{2,1,0:T(8,128)(2,1)}), bf16[4,80,5120]{2,1,0:T(8,128)(2,1)S(1)}, u32[]{:S(2)}, u32[]{:S(2)}) async-start(bf16[4,80,5120]{2,1,0:T(8,128)(2,1)} %get-tuple-element.24), calls=%async_computation.1 | async-start | bytes 6553600 | tf_op jit(solution)/shard_map/all_to_all | solution.py:246
  200.4 362.6 %collective-permute-start = (bf16[20,32,2560]{2,1,0:T(8,128)(2,1)}, bf16[20,32,2560]{2,1,0:T(8,128)(2,1)}, u32[]{:S(2)}, u32[]{:S(2)}) collective-permute-start(bf16[20,32,2560]{2,1,0:T(8,128)(2,1)} %get-tuple-element.21), channel_id=1, source_target_pairs={{0,4},{4,0},{1,5},{5,1},{2,6},{6,2},{3,7},{7,3},{8,12},{12,8},{9,1... | collective-permute-start | bytes 9830408 | tf_op jit(solution)/shard_map/ppermute | solution.py:13
  202.1 8.4 %copy-start.7 = (f32[32,32]{1,0:T(8,128)S(1)}, f32[32,32]{1,0:T(8,128)}, u32[]{:S(2)}) copy-start(f32[32,32]{1,0:T(8,128)} %param.9) | copy-start | bytes 12292
  208.4 362.7 %collective-permute-start.2 = (bf16[40,32,2560]{2,1,0:T(8,128)(2,1)}, bf16[40,32,2560]{2,1,0:T(8,128)(2,1)}, u32[]{:S(2)}, u32[]{:S(2)}) collective-permute-start(bf16[40,32,2560]{2,1,0:T(8,128)(2,1)} %dynamic-slice_bitcast_fusion), channel_id=1, source_target_pairs={{0,4},{4,0},{1,5},{5,1},{2,6},{6,2},{3,7},{7,3},{8,12},{12,8},{9,1... | collective-permute-start | bytes 19660808 | tf_op jit(solution)/shard_map/ppermute | solution.py:13
  208.8 376.2 %collective-permute-start.3 = (bf16[20,32,2560]{2,1,0:T(8,128)(2,1)}, bf16[20,32,2560]{2,1,0:T(8,128)(2,1)}, u32[]{:S(2)}, u32[]{:S(2)}) collective-permute-start(bf16[20,32,2560]{2,1,0:T(8,128)(2,1)} %get-tuple-element.20), channel_id=1, source_target_pairs={{0,4},{4,0},{1,5},{5,1},{2,6},{6,2},{3,7},{7,3},{8,12},{12,8},{9,1... | collective-permute-start | bytes 9830408 | tf_op jit(solution)/shard_map/ppermute | solution.py:13
  230.0 1.7 copy-start.3
  244.1 3.4 copy-start.2
  247.4 305.1 %collective-permute-start.1 = (bf16[4,80,5120]{2,1,0:T(8,128)(2,1)S(1)}, bf16[4,80,5120]{2,1,0:T(8,128)(2,1)}, u32[]{:S(2)}, u32[]{:S(2)}) collective-permute-start(bf16[4,80,5120]{2,1,0:T(8,128)(2,1)S(1)} %copy-done.2), channel_id=1, source_target_pairs={{0,4},{4,0},{1,5},{5,1},{2,6},{6,2},{3,7},{7,3},{8,12},{12,8},{9,1... | collective-permute-start | bytes 9830408 | tf_op jit(solution)/shard_map/ppermute | solution.py:13
  552.5 10.5 %copy-start.5 = (bf16[40,64,640]{2,1,0:T(8,128)(2,1)S(1)}, bf16[40,64,640]{2,1,0:T(8,128)(2,1)}, u32[]{:S(2)}) copy-start(bf16[40,64,640]{2,1,0:T(8,128)(2,1)} %add_convert_fusion) | copy-start | bytes 9830404
  567.6 3.5 slice-start
  589.4 5.7 copy-start.4
  593.0 8.9 %collective-permute-start.5 = (f32[20,2560]{1,0:T(8,128)S(1)}, f32[20,2560]{1,0:T(8,128)S(1)}, u32[]{:S(2)}, u32[]{:S(2)}) collective-permute-start(f32[20,2560]{1,0:T(8,128)S(1)} %broadcast_multiply_fusion.3), channel_id=1, source_target_pairs={{0,4},{4,0},{1,5},{5,1},{2,6},{6,2},{3,7},{7,3},{8,12},{12,8},{9,1... | collective-permute-start | bytes 614408 | tf_op jit(solution)/shard_map/ppermute | solution.py:13
  594.3 17.8 %collective-permute-start.4 = (f32[60,2560]{1,0:T(8,128)S(1)}, f32[60,2560]{1,0:T(8,128)S(1)}, u32[]{:S(2)}, u32[]{:S(2)}) collective-permute-start(f32[60,2560]{1,0:T(8,128)S(1)} %pad_maximum_fusion.5), channel_id=1, source_target_pairs={{0,4},{4,0},{1,5},{5,1},{2,6},{6,2},{3,7},{7,3},{8,12},{12,8},{9,1... | collective-permute-start | bytes 1843208 | tf_op jit(solution)/shard_map/ppermute | solution.py:13
